TPU v7x, 256 devices: a whole 4x4x8 slice. The times are simulated.
256 devices in a mesh: grp: 8 (over y, core), row: 32 (over z, x).
Axes of the slice: x: 4, y: 4, z: 8, core: 2. Of those that a mesh axis runs over, the one named last changes fastest.
Arguments:
- features: bfloat16 [524288, 256], P(('grp', 'row')), may hold values from -6 to 6
- cotangent: bfloat16 [524288, 256], P(('grp', 'row')), may hold values from -6 to 6
- self_weight: bfloat16 [256, 256], replicated, may hold values from -0.375 to 0.375
- neighbor_weight: bfloat16 [256, 256], replicated, may hold values from -0.375 to 0.375
- tile_values: bfloat16 [256, 64, 128, 128], P(('grp', 'row')), may hold values from 0 to 1
- tile_index: int32 [256, 64, 2], P(('grp', 'row')), may hold values from 0 to 15
- hub_adjacency: bfloat16 [524288, 1024], P(('grp', 'row')), may hold values from 0 to 1
- hub_owner: int32 [8, 8], P('grp'), may hold values from 0 to 31
- send_rows: int32 [256, 8, 64], P(('grp', 'row')), may hold values from 0 to 2047
- cut_adjacency: bfloat16 [524288, 512], P(('grp', 'row')), may hold values from 0 to 1
- degrees: int32 [524288], P(('grp', 'row')), may hold values from 1024 to 2047
Outputs:
- hidden: bfloat16 [524288, 256], P(('grp', 'row'))
- grad_features: bfloat16 [524288, 256], P(('grp', 'row'))
- grad_self: float32 [256, 256], replicated
- grad_neighbor: float32 [256, 256], replicated
Inputs may be any that keep to these rules, and one draw needn't show every extreme that they name: `send_rows`: rows may repeat.
All inputs are finite; a program needn't handle non-finite values.
Results may differ from a plain program's by a relative error of at most 0.014.
Values may be sent and summed in bfloat16 or wider, within the bound.
A program may use at most 128 MiB of HBM per device.

v0:
```python
import jax
import jax.numpy as jnp
from jax import lax
from jax.sharding import PartitionSpec as P

TILE = 128
HUB = 128


def spread(value, axis, root):
    mine = lax.axis_index(axis) == root
    return lax.psum(jnp.where(mine, value, jnp.zeros_like(value)), axis)


def on_device(
    features,
    cotangent,
    self_weight,
    neighbor_weight,
    tile_values,
    tile_index,
    hub_adjacency,
    hub_owner,
    send_rows,
    cut_adjacency,
    degrees,
):
    node_count, width = features.shape
    tile_total = node_count // TILE
    group_count = lax.axis_size("grp")
    section_count = hub_owner.shape[1]
    values = tile_values[0]
    index = tile_index[0]
    owners = hub_owner[0]
    blocks = features.reshape(tile_total, TILE, width)
    row_select = (index[:, 0][None, :] == jnp.arange(tile_total)[:, None]).astype(jnp.float32)
    col_select = (index[:, 1][None, :] == jnp.arange(tile_total)[:, None]).astype(jnp.float32)
    picked = blocks[index[:, 1]]
    product = jnp.einsum("lab,lbf->laf", values, picked, preferred_element_type=jnp.float32)
    local_sum = jnp.einsum(
        "nl,laf->naf", row_select, product, precision=lax.Precision.HIGHEST
    ).reshape(node_count, width)
    heads = features[:HUB]
    hub_sum = jnp.zeros((node_count, width), jnp.float32)
    for section in range(section_count):
        panel = spread(heads, "row", owners[section])
        hub_sum = hub_sum + jnp.dot(
            hub_adjacency[:, section * HUB : (section + 1) * HUB],
            panel,
            preferred_element_type=jnp.float32,
        )
    outgoing = features[send_rows[0]]
    arrived = lax.all_to_all(outgoing, "grp", split_axis=0, concat_axis=0, tiled=True)
    cut_sum = jnp.dot(
        cut_adjacency,
        arrived.reshape(group_count * outgoing.shape[1], width),
        preferred_element_type=jnp.float32,
    )
    scaling = lax.rsqrt(degrees.astype(jnp.float32))[:, None]
    aggregated = ((local_sum + hub_sum + cut_sum) * scaling).astype(jnp.bfloat16)
    before = jnp.dot(features, self_weight, preferred_element_type=jnp.float32) + jnp.dot(
        aggregated, neighbor_weight, preferred_element_type=jnp.float32
    )
    activated, pullback = jax.vjp(jax.nn.gelu, before)
    hidden = activated.astype(jnp.bfloat16)
    grad_before = pullback(cotangent.astype(jnp.float32))[0].astype(jnp.bfloat16)
    rows_dims = (((0,), (0,)), ((), ()))
    cols_dims = (((1,), (1,)), ((), ()))
    self_part = lax.dot_general(
        features, grad_before, rows_dims, preferred_element_type=jnp.float32
    )
    neighbor_part = lax.dot_general(
        aggregated, grad_before, rows_dims, preferred_element_type=jnp.float32
    )
    grad_self, grad_neighbor = lax.psum((self_part, neighbor_part), ("grp", "row"))
    grad_aggregate = (
        lax.dot_general(grad_before, neighbor_weight, cols_dims, preferred_element_type=jnp.float32)
        * scaling
    ).astype(jnp.bfloat16)
    grad_total = lax.dot_general(
        grad_before, self_weight, cols_dims, preferred_element_type=jnp.float32
    )
    agg_blocks = grad_aggregate.reshape(tile_total, TILE, width)[index[:, 0]]
    returned = jnp.einsum("lab,laf->lbf", values, agg_blocks, preferred_element_type=jnp.float32)
    grad_total = grad_total + jnp.einsum(
        "nl,lbf->nbf", col_select, returned, precision=lax.Precision.HIGHEST
    ).reshape(node_count, width)
    hub_terms = lax.dot_general(
        hub_adjacency, grad_aggregate, rows_dims, preferred_element_type=jnp.float32
    ).reshape(section_count, HUB, width)
    totals = lax.psum(hub_terms.astype(jnp.bfloat16), "row").astype(jnp.float32)
    owned = (owners == lax.axis_index("row")).astype(jnp.float32)
    hub_grad = jnp.einsum("s,shf->hf", owned, totals, precision=lax.Precision.HIGHEST)
    grad_total = grad_total.at[:HUB].add(hub_grad)
    back_rows = lax.dot_general(
        cut_adjacency, grad_aggregate, rows_dims, preferred_element_type=jnp.float32
    ).astype(jnp.bfloat16)
    back_rows = back_rows.reshape(group_count, -1, width)
    returned_rows = lax.all_to_all(back_rows, "grp", split_axis=0, concat_axis=0, tiled=True)
    scatter_table = (send_rows[0].reshape(-1)[None, :] == jnp.arange(node_count)[:, None]).astype(
        jnp.bfloat16
    )
    grad_total = grad_total + jnp.dot(
        scatter_table, returned_rows.reshape(-1, width), preferred_element_type=jnp.float32
    )
    return (hidden, grad_total.astype(jnp.bfloat16), grad_self, grad_neighbor)


def solution(mesh):
    in_specs = (
        P(("grp", "row"), None),
        P(("grp", "row"), None),
        P(),
        P(),
        P(("grp", "row"), None, None, None),
        P(("grp", "row"), None, None),
        P(("grp", "row"), None),
        P("grp", None),
        P(("grp", "row"), None, None),
        P(("grp", "row"), None),
        P(("grp", "row")),
    )
    out_specs = (P(("grp", "row"), None), P(("grp", "row"), None), P(), P())
    return jax.shard_map(
        on_device, mesh=mesh, in_specs=in_specs, out_specs=out_specs, check_vma=False
    )
```

profile of v0, /device:TPU:1, one launch (start us, length us, event | category | flops | bytes accessed | tf_op | source)
XLA Modules:
  0.0 634.7 jit_solution(11707294678581093016)
XLA Ops:
  7.2 0.8 compare_select_fusion
  8.2 3.6 gather_fusion.1
  11.7 6.6 %all-to-all-start = ((bf16[8,64,256]{2,1,0:T(8,128)(2,1)}), bf16[8,64,256]{2,1,0:T(8,128)(2,1)S(1)}, u32[]{:S(2)}, u32[]{:S(2)}) async-start(bf16[8,64,256]{2,1,0:T(8,128)(2,1)} %bitcast.18), calls=%async_computation | async-start | bytes 524288 | tf_op jit(solution)/shard_map/all_to_all | solution.py:53
  18.3 0.6 fusion.52
  23.9 0.8 broadcast_select_fusion
  24.8 0.6 eq.97
  25.5 0.6 slice_bitcast_fusion
  26.0 2.8 gather_fusion
  28.8 6.8 %fusion.25 = f32[64,256,128]{2,1,0:T(8,128)} fusion(bf16[64,128,256]{2,1,0:T(8,128)(2,1)} %gather_fusion, bf16[1,64,128,128]{3,2,1,0:T(8,128)(2,1)S(1)} %copy-done), kind=kOutput, calls=%fused_computation.44 | convolution fusion | flops 536870912 | bytes 14680064 | tf_op jit(solution)/shard_map/lab,lbf->laf/dot_general | solution.py:39
  35.6 9.2 %copy.25 = f32[64,256,128]{1,0,2:T(8,128)} copy(f32[64,256,128]{2,1,0:T(8,128)} %fusion.25) | data formatting | bytes 16777216 | tf_op jit(solution)/shard_map/lab,lbf->laf/dot_general | solution.py:39
  44.8 5.2 fusion.2
  50.0 2.6 copy.18
  52.6 2.9 copy.19
  55.5 0.7 convert_rsqrt_fusion
  56.2 1.8 fusion.53
  58.0 112.8 %all-reduce.10.cloned.1.call-done = (bf16[128,256]{1,0:T(8,128)(2,1)}, bf16[128,256]{1,0:T(8,128)(2,1)}, bf16[128,256]{1,0:T(8,128)(2,1)}, bf16[128,256]{1,0:T(8...) async-done(((bf16[128,256]{1,0:T(8,128)(2,1)}, bf16[128,256]{1,0:T(8,128)(2,1)}, ...) | async-done | bytes 524304 | tf_op jit(solution)/shard_map/psum | solution.py:12
  170.9 1.6 fusion.37
  172.5 1.6 convolution_add_fusion.8
  174.1 0.7 copy-done.5
  176.5 0.5 convolution_add_fusion.5
  177.3 0.5 convolution_add_fusion.4
  178.2 0.5 convolution_add_fusion.3
  178.7 1.1 copy-done.4
  179.8 1.8 fusion.9
  181.6 3.1 fusion.10
  184.8 3.0 fusion.15
  187.8 1.1 fusion.54
  188.9 1.2 convolution_bitcast_fusion.1
  190.1 2.7 fusion.12
  192.8 1.7 copy.29
  194.5 2.8 gather_fusion.2
  197.3 6.8 %fusion.23 = f32[64,256,128]{2,1,0:T(8,128)} fusion(bf16[64,128,256]{2,1,0:T(8,128)(2,1)} %gather_fusion.2, bf16[1,64,128,128]{3,2,1,0:T(8,128)(2,1)S(1)} %copy-done), kind=kOutput, calls=%fused_computation.42 | convolution fusion | flops 536870912 | bytes 14680064 | tf_op jit(solution)/shard_map/lab,laf->lbf/dot_general | solution.py:84
  204.0 9.2 %copy.27 = f32[64,256,128]{1,0,2:T(8,128)} copy(f32[64,256,128]{2,1,0:T(8,128)} %fusion.23) | data formatting | bytes 16777216 | tf_op jit(solution)/shard_map/lab,laf->lbf/dot_general | solution.py:84
  213.2 5.2 fusion
  218.4 2.6 copy.22
  221.1 3.4 fusion.28
  224.5 0.9 copy.30
  225.5 2.7 fusion.29
  228.2 0.8 copy.23
  229.0 9.7 %all-to-all-start.1 = ((bf16[8,64,256]{2,1,0:T(8,128)(2,1)}), bf16[8,64,256]{2,1,0:T(8,128)(2,1)S(1)}, u32[]{:S(2)}, u32[]{:S(2)}) async-start(bf16[8,64,256]{2,1,0:T(8,128)(2,1)} %bitcast.32), calls=%async_computation.1 | async-start | bytes 524288 | tf_op jit(solution)/shard_map/all_to_all | solution.py:99
  238.7 3.4 convolution_add_fusion
  242.1 232.1 %all-reduce.8.cloned.1.call-done = (f32[256,256]{0,1:T(8,128)}, f32[256,256]{1,0:T(8,128)}) async-done(((f32[256,256]{0,1:T(8,128)}, f32[256,256]{1,0:T(8,128)}), (f32[256,256]{0,1:T(8,128)}, f32[256,256]{1,0:T(8,128)})) %all-reduce.8.cloned.1.call-update) | async-done | bytes 524304 | tf_op jit(solution)/shard_map/psum | solution.py:75
  474.1 1.8 copy.24
  475.9 145.0 %all-reduce.6.cloned.1.call-done = bf16[8,128,256]{1,0,2:T(8,128)(2,1)} async-done(((bf16[8,128,256]{1,0,2:T(8,128)(2,1)}), bf16[8,128,256]{1,0,2:T(8,128)(2,1)}) %all-reduce.6.cloned.1.call-update) | async-done | bytes 524304 | tf_op jit(solution)/shard_map/psum | solution.py:91
  620.9 1.3 fusion.46
  622.4 1.6 fusion.39
  624.0 3.4 fusion.11
  627.4 0.7 copy.43
  (62 shorter events, 2.8 us)
Async XLA Ops:
  7.2 21.7 %copy-start = (bf16[1,64,128,128]{3,2,1,0:T(8,128)(2,1)S(1)}, bf16[1,64,128,128]{3,2,1,0:T(8,128)(2,1)}, u32[]{:S(2)}) copy-start(bf16[1,64,128,128]{3,2,1,0:T(8,128)(2,1)} %param.17) | copy-start | bytes 6291460
  7.2 17.6 %copy-start.20 = (s32[1,8,64]{2,1,0:T(8,128)S(1)}, s32[1,8,64]{2,1,0:T(8,128)}, u32[]{:S(2)}) copy-start(s32[1,8,64]{2,1,0:T(8,128)} %param.21) | copy-start | bytes 6148
  7.2 16.7 %copy-start.1 = (bf16[2048,256]{1,0:T(8,128)(2,1)S(1)}, bf16[2048,256]{1,0:T(8,128)(2,1)}, u32[]{:S(2)}) copy-start(bf16[2048,256]{1,0:T(8,128)(2,1)} %param.13) | copy-start | bytes 3145732
  7.2 11.1 %copy-start.19 = (s32[1,8]{1,0:T(1,128)S(1)}, s32[1,8]{1,0:T(1,128)}, u32[]{:S(2)}) copy-start(s32[1,8]{1,0:T(1,128)} %param.20) | copy-start | bytes 100
  7.2 18.2 %copy-start.23 = (s32[1,64,2]{1,2,0:T(2,128)S(1)}, s32[1,64,2]{1,2,0:T(2,128)}, u32[]{:S(2)}) copy-start(s32[1,64,2]{1,2,0:T(2,128)} %param.18) | copy-start | bytes 1540
  11.7 169.8 %all-to-all-start = ((bf16[8,64,256]{2,1,0:T(8,128)(2,1)}), bf16[8,64,256]{2,1,0:T(8,128)(2,1)S(1)}, u32[]{:S(2)}, u32[]{:S(2)}) async-start(bf16[8,64,256]{2,1,0:T(8,128)(2,1)} %bitcast.18), calls=%async_computation | async-start | bytes 524288 | tf_op jit(solution)/shard_map/all_to_all | solution.py:53
  18.3 152.6 %all-reduce.10.cloned.1.call-start = ((), (), s32[]{:S(2)}) async-start(), calls=%async_computation.4 | async-start | bytes 1048576 | tf_op jit(solution)/shard_map/psum | solution.py:12
  24.8 449.4 %all-reduce.8.cloned.1.call-start = ((), (), s32[]{:S(2)}) async-start(), calls=%async_computation.3 | async-start | bytes 1048576 | tf_op jit(solution)/shard_map/psum | solution.py:75
  52.6 3.6 copy-start.8
  170.9 1.6 copy-start.18
  172.5 2.4 copy-start.5
  172.5 2.4 copy-start.17
  174.8 0.8 copy-start.16
  175.7 0.8 copy-start.15
  176.5 0.8 copy-start.14
  177.3 0.8 copy-start.13
  178.2 1.6 copy-start.4
  178.2 1.6 copy-start.12
  181.6 3.2 copy-start.7
  181.6 3.2 copy-start.10
  181.6 3.2 copy-start.24
  187.8 1.1 copy-start.2
  187.8 2.3 copy-start.11
  204.0 9.2 %copy-start.22 = (s32[64]{0:T(128)S(1)}, s32[64]{0:T(128)}, u32[]{:S(2)}) copy-start(s32[64]{0:T(128)} %get-tuple-element.44) | copy-start | bytes 772
  218.4 2.7 copy-start.6
  221.0 399.9 %all-reduce.6.cloned.1.call-start = ((), (), s32[]{:S(2)}) async-start(), calls=%async_computation.2 | async-start | bytes 1048576 | tf_op jit(solution)/shard_map/psum | solution.py:91
  225.4 13.2 %copy-start.3 = (bf16[2048,256]{1,0:T(8,128)(2,1)S(1)}, bf16[2048,256]{1,0:T(8,128)(2,1)}, u32[]{:S(2)}) copy-start(bf16[2048,256]{1,0:T(8,128)(2,1)} %copy-done.2) | copy-start | bytes 3145732
  229.0 395.0 %all-to-all-start.1 = ((bf16[8,64,256]{2,1,0:T(8,128)(2,1)}), bf16[8,64,256]{2,1,0:T(8,128)(2,1)S(1)}, u32[]{:S(2)}, u32[]{:S(2)}) async-start(bf16[8,64,256]{2,1,0:T(8,128)(2,1)} %bitcast.32), calls=%async_computation.1 | async-start | bytes 524288 | tf_op jit(solution)/shard_map/all_to_all | solution.py:99
  238.7 385.3 %copy-start.21 = (s32[512]{0:T(512)S(1)}, s32[512]{0:T(512)}, u32[]{:S(2)}) copy-start(s32[512]{0:T(512)} %eq.97) | copy-start | bytes 6148
  622.3 5.1 copy-start.9
Sparse Core Ops, SparseCore 0:
  24.9 145.9 all-reduce.9
  221.1 252.9 all-reduce.7
  477.9 142.9 all-reduce.5
where the time goes:
time: 640 us; the launch traced here: 635 us
  waiting for transfers between devices  490 us (77%)
  matrix products  58.4 us (9%)
  local copies, waits for them, and re-layouts  46.5 us (7%)
  between operations  19 us (3%)
  starting transfers between devices  16.3 us (3%)
    psum x1, waiting for transfers between devices, on_device(): lax.psum((self_part, neighbor_part), ('grp', 'row'))  232 us
    psum x1, waiting for transfers between devices, on_device(): totals = lax.psum(hub_terms.astype(jnp.bfloat16), 'row').astype(jnp.float32)  145 us
    psum x1, waiting for transfers between devices, spread(): return lax.psum(jnp.where(mine, value, jnp.zeros_like(value)), axis)  113 us
  transfers between devices with their start and end apart: 5, of which 3 were waited for; matrix products, arithmetic and copies ran while one was open for 9% of the time, Pallas kernels for 0%

commit v1 on v0

v1 whole, which is shorter than its diff:
```python
import jax
import jax.numpy as jnp
from jax import lax
from jax.experimental import pallas as pl
from jax.experimental.pallas import tpu as pltpu
from jax.sharding import PartitionSpec as P

TILE = 128
HUB = 128
ACROSS = 4
CHUNK = 256
F32 = jnp.float32
BF16 = jnp.bfloat16
VMEM = pl.BlockSpec(memory_space=pltpu.VMEM)
SMEM = pl.BlockSpec(memory_space=pltpu.SMEM)
MESH = pl.DeviceIdType.MESH


def dot(left, right):
    return jnp.dot(left, right, preferred_element_type=F32)


def dot_cols(left, right):
    return lax.dot_general(left, right, (((1,), (1,)), ((), ())), preferred_element_type=F32)


class Place:
    def __init__(self):
        self.row = lax.axis_index("row")
        self.grp = lax.axis_index("grp")
        self.groups = lax.axis_size("grp")
        self.depth = lax.axis_size("row") // ACROSS
        self.x = lax.rem(self.row, ACROSS)
        self.z = lax.div(self.row, ACROSS)

    def along_x(self, shift):
        peer = lax.rem(self.x + shift, ACROSS)
        return peer, {"row": self.z * ACROSS + peer}

    def along_z(self, shift):
        peer = lax.rem(self.z + shift, self.depth)
        return peer, {"row": peer * ACROSS + self.x}

    def along_grp(self, shift):
        peer = lax.rem(self.grp + shift, self.groups)
        return peer, {"grp": peer}

    def greet(self):
        barrier = pltpu.get_barrier_semaphore()
        count = 0
        for peers, size in (
            (self.along_x, ACROSS),
            (self.along_z, self.depth),
            (self.along_grp, self.groups),
        ):
            for shift in range(1, size):
                pl.semaphore_signal(
                    barrier, inc=1, device_id=peers(shift)[1], device_id_type=MESH
                )
                count += 1
        pl.semaphore_wait(barrier, count)


def send_all(peers, size, source, target, sems):
    send, recv = sems
    copies = []
    for shift in range(1, size):
        peer, device = peers(shift)
        copy = pltpu.make_async_remote_copy(
            src_ref=source(peer, shift),
            dst_ref=target(shift),
            send_sem=send.at[shift - 1],
            recv_sem=recv.at[shift - 1],
            device_id=device,
            device_id_type=MESH,
        )
        copy.start()
        copies.append(copy)
    return copies


def arrive(copies):
    for copy in copies:
        copy.wait_recv()


def forward_exchange(
    mask_ref, heads_ref, outgoing_ref, panels_ref, arrived_ref, near, part, pieces, panel, cut, *sems
):
    here = Place()
    depth, groups = here.depth, here.groups
    pairs = [(sems[2 * k], sems[2 * k + 1]) for k in range(5)]
    each = mask_ref.shape[0] // ACROSS
    per = depth // each
    here.greet()
    heads_out = send_all(
        here.along_x, ACROSS, lambda p, d: heads_ref, lambda d: near.at[d - 1], pairs[0]
    )
    cut_out = send_all(
        here.along_grp, groups, lambda p, d: outgoing_ref.at[p], lambda d: cut.at[here.grp], pairs[1]
    )
    cut[here.grp] = outgoing_ref[here.grp]
    arrive(heads_out)
    for j in range(each):
        section = here.x * each + j
        total = heads_ref[...].astype(F32) * mask_ref[section, here.row]
        for shift in range(1, ACROSS):
            sender = here.z * ACROSS + lax.rem(here.x + ACROSS - shift, ACROSS)
            total += near[shift - 1].astype(F32) * mask_ref[section, sender]
        part[pl.ds(j * per, per)] = total.astype(BF16).reshape(per, HUB // per, -1)
    parts_out = send_all(
        here.along_z, depth, lambda p, d: part.at[p], lambda d: pieces.at[d - 1], pairs[2]
    )
    arrive(parts_out)
    total = part[here.z].astype(F32)
    for shift in range(1, depth):
        total += pieces[shift - 1].astype(F32)
    panel[here.x, here.z] = total.astype(BF16)
    mine = panel.at[here.x, here.z]
    pieces_out = send_all(here.along_z, depth, lambda p, d: mine, lambda d: mine, pairs[3])
    arrive(pieces_out)
    block = panel.at[here.x]
    panels_out = send_all(here.along_x, ACROSS, lambda p, d: block, lambda d: block, pairs[4])
    arrive(cut_out)
    arrived_ref[...] = cut[...]
    arrive(panels_out)
    panels_ref[...] = panel[...]
    for copy in heads_out + cut_out + parts_out + pieces_out + panels_out:
        copy.wait_send()


def backward_exchange(
    mask_ref,
    hub_ref,
    back_ref,
    weight_ref,
    hub_grad_ref,
    returned_ref,
    sum_ref,
    near,
    part,
    pieces,
    whole,
    owned,
    owned_near,
    cut,
    w_near,
    w_part,
    w_pieces,
    w_across,
    w_block,
    w_whole,
    *sems,
):
    here = Place()
    depth, groups = here.depth, here.groups
    pairs = [(sems[2 * k], sems[2 * k + 1]) for k in range(10)]
    each = mask_ref.shape[0] // ACROSS
    per = depth // each
    here.greet()
    sent = []

    def send(*args):
        copies = send_all(*args)
        sent.extend(copies)
        return copies

    hub_out = send(
        here.along_x, ACROSS, lambda p, d: hub_ref.at[p], lambda d: near.at[d - 1], pairs[0]
    )
    weight_out = send(
        here.along_grp, groups, lambda p, d: weight_ref.at[p], lambda d: w_near.at[d - 1], pairs[1]
    )
    cut_out = send(
        here.along_grp, groups, lambda p, d: back_ref.at[p], lambda d: cut.at[here.grp], pairs[2]
    )
    cut[here.grp] = back_ref[here.grp]

    arrive(hub_out)
    total = hub_ref[here.x].astype(F32)
    for shift in range(1, ACROSS):
        total += near[shift - 1].astype(F32)
    part[...] = total.astype(BF16).reshape(part.shape)
    parts_out = send(
        here.along_z, depth, lambda p, d: part.at[p], lambda d: pieces.at[d - 1], pairs[3]
    )

    arrive(weight_out)
    total = weight_ref[here.grp]
    for shift in range(1, groups):
        total += w_near[shift - 1]
    w_part[...] = total.reshape(w_part.shape)
    w_parts_out = send(
        here.along_z, depth, lambda p, d: w_part.at[p], lambda d: w_pieces.at[d - 1], pairs[4]
    )

    arrive(parts_out)
    total = part[here.z].astype(F32)
    for shift in range(1, depth):
        total += pieces[shift - 1].astype(F32)
    whole[here.z] = total.astype(BF16)
    mine = whole.at[here.z]
    whole_out = send(here.along_z, depth, lambda p, d: mine, lambda d: mine, pairs[5])

    arrive(w_parts_out)
    total = w_part[here.z]
    for shift in range(1, depth):
        total += w_pieces[shift - 1]
    w_across[here.x] = total
    w_mine = w_across.at[here.x]
    w_across_out = send(here.along_x, ACROSS, lambda p, d: w_mine, lambda d: w_mine, pairs[6])

    def owned_by(row):
        total = 0.0
        for j in range(each):
            terms = whole[pl.ds(j * per, per)].astype(F32).reshape(HUB, -1)
            total += terms * mask_ref[here.x * each + j, row]
        return total

    arrive(whole_out)
    for shift in range(1, ACROSS):
        peer = here.z * ACROSS + lax.rem(here.x + shift, ACROSS)
        owned[shift - 1] = owned_by(peer).astype(BF16)
    owned_out = send(
        here.along_x, ACROSS, lambda p, d: owned.at[d - 1], lambda d: owned_near.at[d - 1], pairs[7]
    )

    arrive(w_across_out)
    total = w_across[0]
    for k in range(1, ACROSS):
        total += w_across[k]
    w_block[here.z] = total
    w_piece = w_block.at[here.z]
    w_block_out = send(here.along_z, depth, lambda p, d: w_piece, lambda d: w_piece, pairs[8])

    arrive(w_block_out)
    w_whole[here.grp] = w_block[...].reshape(w_whole.shape[1:])
    w_last = w_whole.at[here.grp]
    w_whole_out = send(here.along_grp, groups, lambda p, d: w_last, lambda d: w_last, pairs[9])

    arrive(owned_out)
    total = owned_by(here.row)
    for shift in range(1, ACROSS):
        total += owned_near[shift - 1].astype(F32)
    hub_grad_ref[...] = total
    arrive(cut_out)
    returned_ref[...] = cut[...]
    arrive(w_whole_out)
    sum_ref[...] = w_whole[...]
    for copy in sent:
        copy.wait_send()


def pair_sems(*counts):
    return [pltpu.SemaphoreType.DMA((n - 1,)) for n in counts for _ in range(2)]


def gather_rows(rows_ref, features_ref, out_ref):
    nodes = features_ref.shape[0]
    for start in range(0, out_ref.shape[0], TILE):
        spot = lax.broadcasted_iota(jnp.int32, (TILE, nodes), 1)
        table = jnp.where(spot == rows_ref[start : start + TILE, :], 1.0, 0.0).astype(BF16)
        out_ref[start : start + TILE, :] = dot(table, features_ref[...]).astype(BF16)


def layer_kernel(
    index_ref,
    features_ref,
    cotangent_ref,
    self_ref,
    neighbor_ref,
    values_ref,
    hub_ref,
    panels_ref,
    cut_ref,
    arrived_ref,
    scale_ref,
    hidden_ref,
    total_ref,
    hub_out,
    back_out,
    weight_out,
    acc,
    grads,
    sides,
    hub_acc,
    back_acc,
    self_acc,
    neighbor_acc,
):
    nodes, width = features_ref.shape
    tiles = values_ref.shape[0]
    per = CHUNK // TILE

    def begin(c, carry):
        rows = pl.ds(pl.multiple_of(c * CHUNK, CHUNK), CHUNK)
        acc[rows, :] = dot(hub_ref[rows, :], panels_ref[...]) + dot(
            cut_ref[rows, :], arrived_ref[...]
        )
        return carry

    lax.fori_loop(0, nodes // CHUNK, begin, 0)

    def gather_tile(t, carry):
        rows = pl.ds(pl.multiple_of(index_ref[2 * t] * TILE, TILE), TILE)
        cols = pl.ds(pl.multiple_of(index_ref[2 * t + 1] * TILE, TILE), TILE)
        acc[rows, :] += dot(values_ref[t], features_ref[cols, :])
        return carry

    lax.fori_loop(0, tiles, gather_tile, 0, unroll=4)

    hub_acc[...] = jnp.zeros_like(hub_acc)
    back_acc[...] = jnp.zeros_like(back_acc)
    self_acc[...] = jnp.zeros_like(self_acc)
    neighbor_acc[...] = jnp.zeros_like(neighbor_acc)
    sides[...] = jnp.zeros_like(sides)

    def dense(c, carry):
        rows = pl.ds(pl.multiple_of(c * CHUNK, CHUNK), CHUNK)
        scale = scale_ref[rows, :]
        own = features_ref[rows, :]
        aggregated = (acc[rows, :] * scale).astype(BF16)
        before = dot(own, self_ref[...]) + dot(aggregated, neighbor_ref[...])
        root = 0.7978845608028654
        square = before * before
        bend = jnp.tanh(root * before * (1.0 + 0.044715 * square))
        half = 0.5 * (1.0 + bend)
        hidden_ref[rows, :] = (before * half).astype(BF16)
        slope = half + 0.5 * before * (1.0 - bend * bend) * (
            root * (1.0 + 3.0 * 0.044715 * square)
        )
        grad_before = (cotangent_ref[rows, :].astype(F32) * slope).astype(BF16)
        turned = grad_before.T
        self_acc[...] += dot(turned, own)
        neighbor_acc[...] += dot(turned, aggregated)
        total_ref[rows, :] = dot_cols(grad_before, self_ref[...])
        grad_aggregate = (dot_cols(grad_before, neighbor_ref[...]) * scale).astype(BF16)
        turned = grad_aggregate.T
        for k in range(per):
            grads[c * per + k] = turned[:, k * TILE : (k + 1) * TILE]
        hub_acc[...] += dot(turned, hub_ref[rows, :])
        back_acc[...] += dot(turned, cut_ref[rows, :])
        return carry

    lax.fori_loop(0, nodes // CHUNK, dense, 0)

    def return_tile(t, carry):
        sides[index_ref[2 * t + 1]] += dot(grads[index_ref[2 * t]], values_ref[t])
        return carry

    lax.fori_loop(0, tiles, return_tile, 0, unroll=4)

    def finish(k, carry):
        rows = pl.ds(pl.multiple_of(k * TILE, TILE), TILE)
        total_ref[rows, :] += sides[k].T
        return carry

    lax.fori_loop(0, nodes // TILE, finish, 0)
    hub_out[...] = hub_acc[...].T.astype(BF16)
    back_out[...] = back_acc[...].T.astype(BF16)
    weight_out[:width, :] = self_acc[...].T
    weight_out[width:, :] = neighbor_acc[...].T


def final_kernel(rows_ref, total_ref, hub_ref, returned_ref, out_ref):
    count = rows_ref.shape[1]
    for start in range(0, out_ref.shape[0], CHUNK):
        spot = lax.broadcasted_iota(jnp.int32, (CHUNK, count), 0) + start
        table = jnp.where(spot == rows_ref[...], 1.0, 0.0).astype(BF16)
        total = total_ref[start : start + CHUNK, :] + dot(table, returned_ref[...])
        if start == 0:
            out_ref[:HUB, :] = (total[:HUB] + hub_ref[...]).astype(BF16)
            out_ref[HUB:CHUNK, :] = total[HUB:].astype(BF16)
        else:
            out_ref[start : start + CHUNK, :] = total.astype(BF16)


def shape(dims, dtype):
    return jax.ShapeDtypeStruct(dims, dtype)


def on_device(
    features,
    cotangent,
    self_weight,
    neighbor_weight,
    tile_values,
    tile_index,
    hub_adjacency,
    hub_owner,
    send_rows,
    cut_adjacency,
    degrees,
):
    nodes, width = features.shape
    tiles = nodes // TILE
    groups = lax.axis_size("grp")
    members = lax.axis_size("row")
    depth = members // ACROSS
    sections = hub_owner.shape[1]
    sent = send_rows.shape[2]
    arrivals = groups * sent
    block = sections // ACROSS * HUB
    piece = block // depth
    rows = send_rows[0].reshape(-1)
    mask = (hub_owner[0][:, None] == jnp.arange(members)[None, :]).astype(F32)

    outgoing = pl.pallas_call(
        gather_rows,
        out_shape=shape((arrivals, width), BF16),
        in_specs=[VMEM, VMEM],
        out_specs=VMEM,
        name="gather_rows",
    )(rows[:, None], features)

    panels, arrived = pl.pallas_call(
        forward_exchange,
        out_shape=(
            shape((ACROSS, depth, piece, width), BF16),
            shape((groups, sent, width), BF16),
        ),
        in_specs=[SMEM, VMEM, VMEM],
        out_specs=(VMEM, VMEM),
        scratch_shapes=[
            pltpu.VMEM((ACROSS - 1, HUB, width), BF16),
            pltpu.VMEM((depth, piece, width), BF16),
            pltpu.VMEM((depth - 1, piece, width), BF16),
            pltpu.VMEM((ACROSS, depth, piece, width), BF16),
            pltpu.VMEM((groups, sent, width), BF16),
            *pair_sems(ACROSS, groups, depth, depth, ACROSS),
        ],
        compiler_params=pltpu.CompilerParams(collective_id=0, has_side_effects=True),
        name="forward_exchange",
    )(mask, features[:HUB], outgoing.reshape(groups, sent, width))

    scaling = lax.rsqrt(degrees.astype(F32))[:, None]
    hidden, total, hub_terms, back_rows, weights = pl.pallas_call(
        layer_kernel,
        out_shape=(
            shape((nodes, width), BF16),
            shape((nodes, width), F32),
            shape((sections * HUB, width), BF16),
            shape((arrivals, width), BF16),
            shape((2 * width, width), F32),
        ),
        in_specs=[SMEM] + [VMEM] * 10,
        out_specs=(VMEM,) * 5,
        scratch_shapes=[
            pltpu.VMEM((nodes, width), F32),
            pltpu.VMEM((tiles, width, TILE), BF16),
            pltpu.VMEM((tiles, width, TILE), F32),
            pltpu.VMEM((width, sections * HUB), F32),
            pltpu.VMEM((width, arrivals), F32),
            pltpu.VMEM((width, width), F32),
            pltpu.VMEM((width, width), F32),
        ],
        name="layer",
    )(
        tile_index[0].reshape(-1),
        features,
        cotangent,
        self_weight,
        neighbor_weight,
        tile_values[0],
        hub_adjacency,
        panels.reshape(sections * HUB, width),
        cut_adjacency,
        arrived.reshape(arrivals, width),
        scaling,
    )

    wide = 2 * width // groups
    thin = wide // depth
    hub_grad, returned, weights = pl.pallas_call(
        backward_exchange,
        out_shape=(
            shape((HUB, width), F32),
            shape((groups, sent, width), BF16),
            shape((groups, wide, width), F32),
        ),
        in_specs=[SMEM, VMEM, VMEM, VMEM],
        out_specs=(VMEM,) * 3,
        scratch_shapes=[
            pltpu.VMEM((ACROSS - 1, block, width), BF16),
            pltpu.VMEM((depth, piece, width), BF16),
            pltpu.VMEM((depth - 1, piece, width), BF16),
            pltpu.VMEM((depth, piece, width), BF16),
            pltpu.VMEM((ACROSS - 1, HUB, width), BF16),
            pltpu.VMEM((ACROSS - 1, HUB, width), BF16),
            pltpu.VMEM((groups, sent, width), BF16),
            pltpu.VMEM((groups - 1, wide, width), F32),
            pltpu.VMEM((depth, thin, width), F32),
            pltpu.VMEM((depth - 1, thin, width), F32),
            pltpu.VMEM((ACROSS, thin, width), F32),
            pltpu.VMEM((depth, thin, width), F32),
            pltpu.VMEM((groups, wide, width), F32),
            *pair_sems(
                ACROSS, groups, groups, depth, depth, depth, ACROSS, ACROSS, depth, groups
            ),
        ],
        compiler_params=pltpu.CompilerParams(collective_id=1, has_side_effects=True),
        name="backward_exchange",
    )(
        mask,
        hub_terms.reshape(ACROSS, block, width),
        back_rows.reshape(groups, sent, width),
        weights.reshape(groups, wide, width),
    )

    grad_features = pl.pallas_call(
        final_kernel,
        out_shape=shape((nodes, width), BF16),
        in_specs=[VMEM] * 4,
        out_specs=VMEM,
        name="final",
    )(rows[None, :], total, hub_grad, returned.reshape(arrivals, width))
    weights = weights.reshape(2 * width, width)
    return (hidden, grad_features, weights[:width], weights[width:])


def solution(mesh):
    in_specs = (
        P(("grp", "row"), None),
        P(("grp", "row"), None),
        P(),
        P(),
        P(("grp", "row"), None, None, None),
        P(("grp", "row"), None, None),
        P(("grp", "row"), None),
        P("grp", None),
        P(("grp", "row"), None, None),
        P(("grp", "row"), None),
        P(("grp", "row")),
    )
    out_specs = (P(("grp", "row"), None), P(("grp", "row"), None), P(), P())
    return jax.shard_map(
        on_device, mesh=mesh, in_specs=in_specs, out_specs=out_specs, check_vma=False
    )
```

time: 640 us -> 116 us (0.18)
  waiting for transfers between devices: 490 us -> 0 us
  Pallas kernels: 0 us -> 107 us
  matrix products: 58.4 us -> 0 us
  local copies, waits for them, and re-layouts: 46.5 us -> 6.67 us
  between operations: 19 us -> 0.7 us
  starting transfers between devices: 16.3 us -> 0 us
    psum x3 -> x0, waiting for transfers between devices: 490 us -> none  [the longest x1 232 us: on_device(): lax.psum((self_part, neighbor_part), ('grp', 'row'))]
    pallas_call x0 -> x5, Pallas kernels: none -> 107 us  [the longest x1 42.1 us: on_device(): pl.pallas_call(backward_exchange, out_shape=(shape((HUB, width), F32), sh...]
    dot_general x23 -> x0, matrix products: 58.4 us -> none  [the longest x8 7.35 us: on_device(): jnp.dot(hub_adjacency[:, section * HUB:(section + 1) * HUB], panel, prefe...]
    dot_general x5 -> x0, local copies, waits for them, and re-layouts: 23.7 us -> none  [the longest x1 9.22 us: on_device(): jnp.einsum('lab,lbf->laf', values, picked, preferred_element_type=jnp.flo...]
    all_to_all x2 -> x0, starting transfers between devices: 16.2 us -> none  [the longest x1 9.67 us: on_device(): lax.all_to_all(back_rows, 'grp', split_axis=0, concat_axis=0, tiled=True)]
    gather x3 -> x0, local copies, waits for them, and re-layouts: 9.2 us -> none  [the longest x1 3.59 us: on_device(): outgoing = features[send_rows[0]]]
    unnamed x53 -> x9, local copies, waits for them, and re-layouts: 6.73 us -> 0.11 us
  transfers between devices with their start and end apart: 5 -> 0, of which waited for: 3 -> 0; matrix products, arithmetic and copies ran while one was open for 9% -> 0% of each run, Pallas kernels for 0% -> 0%
where the time goes in v1:
time: 116 us; the launch traced here: 115 us
  Pallas kernels  107 us (92%)
  local copies, waits for them, and re-layouts  6.67 us (6%)
  other arithmetic  1.34 us (1%)
    pallas_call x1, Pallas kernels, on_device(): pl.pallas_call(backward_exchange, out_shape=(shape((HUB, width), F32), sh...  42.1 us
    pallas_call x1, Pallas kernels, on_device(): pl.pallas_call(forward_exchange, out_shape=(shape((ACROSS, depth, piece,...  30.2 us
    pallas_call x1, Pallas kernels, on_device(): pl.pallas_call(layer_kernel, out_shape=(shape((nodes, width), BF16), shap...  28.2 us
    pallas_call x1, Pallas kernels, on_device(): pl.pallas_call(final_kernel, out_shape=shape((nodes, width), BF16), in_sp...  3.32 us
    pallas_call x1, Pallas kernels, on_device(): pl.pallas_call(gather_rows, out_shape=shape((arrivals, width), BF16), in_...  2.77 us

profile of v1, /device:TPU:1, one launch (start us, length us, event | category | flops | bytes accessed | tf_op | source)
XLA Modules:
  0.0 115.3 jit_solution(10381991201722048348)
XLA Ops:
  0.6 0.0 copy-start.2
  0.6 0.0 copy-start.3
  0.7 1.3 %fusion.mask_ref = f32[8,32]{1,0:T(8,128)} fusion(s32[8]{0:T(128)} %bitcast.23), kind=kLoop, calls=%fused_computation.2 | loop fusion | flops 512 | bytes 1056 | tf_op jit(solution)/shard_map/convert_element_type | solution.py:406
  2.0 1.6 %broadcast_in_dim_reshape_squeeze.8.rows_ref = s32[512,1]{1,0:T(8,128)} reshape(s32[1,8,64]{2,1,0:T(8,128)} %param.19) | data formatting | bytes 4096 | tf_op jit(solution)/shard_map/broadcast_in_dim;reshape;squeeze | solution.py:414
  3.6 2.8 %gather_rows.1 = bf16[512,256]{1,0:T(8,128)(2,1)} custom-call(s32[512,1]{1,0:T(8,128)} %broadcast_in_dim_reshape_squeeze.8.rows_ref, bf16[2048,256]{1,0:T(8,128)(2,1)} %features_ref.3), custom_call_target="tpu_custom_call" | custom-call | tf_op jit(solution)/shard_map/gather_rows/pallas_call | solution.py:408
  6.3 1.5 %slice.15.heads_ref = bf16[128,256]{1,0:T(8,128)(2,1)} slice(bf16[2048,256]{1,0:T(8,128)(2,1)} %features_ref.3), slice={[0:128], [0:256]} | slice | bytes 131072 | tf_op jit(solution)/shard_map/slice | solution.py:434
  7.8 30.2 %forward_exchange.1 = (bf16[4,8,32,256]{3,2,1,0:T(8,128)(2,1)}, bf16[8,64,256]{2,1,0:T(8,128)(2,1)}) custom-call(f32[8,32]{1,0:T(8,128)} %fusion.mask_ref, bf16[128,256]{1,0:T(8,128)(2,1)} %slice.15.heads_ref, bf16[8,64,256]{2,1,0:T(8,128)(2,1)} %bitcast.13), custom_call_target="tpu_custom_call" | custom-call | tf_op jit(solution)/shard_map/forward_exchange/pallas_call | solution.py:416
  38.1 0.0 copy-done.2
  38.1 1.3 %copy.18.scale_ref = f32[2048,1]{1,0:T(8,128)} copy(f32[2048,1]{0,1:T(1,128)S(1)} %bitcast.22) | data formatting | bytes 16384 | tf_op jit(solution)/shard_map/broadcast_in_dim | solution.py:436
  39.4 0.0 copy-done.3
  39.4 0.1 copy.16
  39.5 0.7 reshape_squeeze.3.index_ref
  40.2 0.0 copy-start.1
  40.2 28.2 %layer.1 = (bf16[2048,256]{1,0:T(8,128)(2,1)}, f32[2048,256]{1,0:T(8,128)}, bf16[1024,256]{1,0:T(8,128)(2,1)}, bf16[512,256]{1,0:T(8,128)(2,1)}, f32[512,256]{1,0:T(8,128)}) custom-call(s32[128]{0:T(128)} %reshape_squeeze.3.index_ref, bf16[2048,256]{1,0:T(8,128)(2,1)} %features_ref.3, bf16[2048,256]{1,0:T(8,128)(2,1)} %cotangent_ref.1, ...), custom_call_target="tpu_custom_call" | custom-call | tf_op jit(solution)/shard_map/layer/pallas_call | solution.py:437
  68.4 42.1 %backward_exchange.1 = (f32[128,256]{1,0:T(8,128)}, bf16[8,64,256]{2,1,0:T(8,128)(2,1)}, f32[8,64,256]{2,1,0:T(8,128)}) custom-call(f32[8,32]{1,0:T(8,128)} %fusion.mask_ref, bf16[4,256,256]{2,1,0:T(8,128)(2,1)} %bitcast.15, bf16[8,64,256]{2,1,0:T(8,128)(2,1)} %bitcast.18, f32[8,64,256]{2,1,0:T(8,128)} %bitcast.16), custom_call_target="tpu_custom_call" | custom-call | tf_op jit(solution)/shard_map/backward_exchange/pallas_call | solution.py:474
  110.4 0.0 copy-start
  110.4 0.0 copy-done.1
  110.5 0.7 broadcast_in_dim_reshape_squeeze.7.rows_ref
  111.1 3.3 %final.1 = bf16[2048,256]{1,0:T(8,128)(2,1)} custom-call(s32[1,512]{1,0:T(1,128)} %broadcast_in_dim_reshape_squeeze.7.rows_ref, f32[2048,256]{1,0:T(8,128)} %get-tuple-element.17.total_ref, f32[128,256]{1,0:T(8,128)} %get-tuple-element.21.hub_ref, bf16[512,256]{1,0:T(8,128)(2,1)} %bitcast.19), custom_call_target="tpu_custom_call" | custom-call | tf_op jit(solution)/shard_map/final/pallas_call | solution.py:510
  114.4 0.0 copy-done
  114.4 0.8 fusion.1
  (1 shorter events, 0.0 us)
Async XLA Ops:
  0.6 37.4 %copy-start.2 = (s32[2048]{0:T(1024)S(1)}, s32[2048]{0:T(1024)}, u32[]{:S(2)}) copy-start(s32[2048]{0:T(1024)} %param.21) | copy-start | bytes 24580
  0.6 38.8 %copy-start.3 = (s32[1,64,2]{1,2,0:T(2,128)S(1)}, s32[1,64,2]{1,2,0:T(2,128)}, u32[]{:S(2)}) copy-start(s32[1,64,2]{1,2,0:T(2,128)} %param.16) | copy-start | bytes 1540
  40.2 70.3 %copy-start.1 = (s32[1,8,64]{2,1,0:T(8,128)S(1)}, s32[1,8,64]{2,1,0:T(8,128)}, u32[]{:S(2)}) copy-start(s32[1,8,64]{2,1,0:T(8,128)} %param.19) | copy-start | bytes 6148
  110.4 4.0 %copy-start = (f32[8,64,256]{2,1,0:T(8,128)S(1)}, f32[8,64,256]{2,1,0:T(8,128)}, u32[]{:S(2)}) copy-start(f32[8,64,256]{2,1,0:T(8,128)} %get-tuple-element.23) | copy-start | bytes 1572868

commit v2 on v0

v2 whole, which is shorter than its diff:
```python
import jax
import jax.numpy as jnp
from jax import lax
from jax.experimental import pallas as pl
from jax.experimental.pallas import tpu as pltpu
from jax.sharding import PartitionSpec as P

TILE = 128
HUB = 128
ACROSS = 4
CHUNK = 256
F32 = jnp.float32
BF16 = jnp.bfloat16
VMEM = pl.BlockSpec(memory_space=pltpu.VMEM)
SMEM = pl.BlockSpec(memory_space=pltpu.SMEM)
MESH = pl.DeviceIdType.MESH


def dot(left, right):
    return jnp.dot(left, right, preferred_element_type=F32)


def dot_cols(left, right):
    return lax.dot_general(left, right, (((1,), (1,)), ((), ())), preferred_element_type=F32)


class Place:
    def __init__(self):
        self.row = lax.axis_index("row")
        self.grp = lax.axis_index("grp")
        self.groups = lax.axis_size("grp")
        self.depth = lax.axis_size("row") // ACROSS
        self.x = lax.rem(self.row, ACROSS)
        self.z = lax.div(self.row, ACROSS)

    def along_x(self, shift):
        peer = lax.rem(self.x + shift, ACROSS)
        return peer, {"row": self.z * ACROSS + peer}

    def along_z(self, shift):
        peer = lax.rem(self.z + shift, self.depth)
        return peer, {"row": peer * ACROSS + self.x}

    def along_grp(self, shift):
        peer = lax.rem(self.grp + shift, self.groups)
        return peer, {"grp": peer}

    def greet(self):
        barrier = pltpu.get_barrier_semaphore()
        count = 0
        for peers, size in (
            (self.along_x, ACROSS),
            (self.along_z, self.depth),
            (self.along_grp, self.groups),
        ):
            for shift in range(1, size):
                pl.semaphore_signal(
                    barrier, inc=1, device_id=peers(shift)[1], device_id_type=MESH
                )
                count += 1
        pl.semaphore_wait(barrier, count)


def send_all(peers, size, source, target, sems):
    send, recv = sems
    copies = []
    for shift in range(1, size):
        peer, device = peers(shift)
        copy = pltpu.make_async_remote_copy(
            src_ref=source(peer, shift),
            dst_ref=target(shift),
            send_sem=send.at[shift - 1],
            recv_sem=recv.at[shift - 1],
            device_id=device,
            device_id_type=MESH,
        )
        copy.start()
        copies.append(copy)
    return copies


def arrive(copies):
    for copy in copies:
        copy.wait_recv()


def chain_tiles(index_ref, owner_ref, links_ref, mask_ref):
    count = index_ref.shape[1]
    lines = (links_ref.shape[0] - 2 * count) // 2

    for side in range(2):
        base = side * (count + lines)

        def clear(k, carry):
            links_ref[base + count + k] = count
            return carry

        def follow(t, carry):
            line = base + count + index_ref[side, t]
            links_ref[base + t] = links_ref[line]
            links_ref[line] = t
            return carry

        lax.fori_loop(0, lines, clear, 0, unroll=True)
        lax.fori_loop(0, count, follow, 0, unroll=4)

    sections, members = mask_ref.shape

    def blank(k, carry):
        for section in range(sections):
            mask_ref[section, k] = 0.0
        return carry

    lax.fori_loop(0, members, blank, 0, unroll=4)
    for section in range(sections):
        mask_ref[section, owner_ref[0, section]] = 1.0


def sage_kernel(
    index_ref,
    links_ref,
    mask_ref,
    columns_ref,
    degrees_ref,
    self_ref,
    neighbor_ref,
    features_hbm,
    cotangent_hbm,
    values_hbm,
    hub_hbm,
    cut_hbm,
    both_ref,
    sum_ref,
    features_ref,
    cotangent_ref,
    values_ref,
    hub_ref,
    cut_ref,
    scale_ref,
    total_ref,
    slots,
    sides,
    acc,
    grads_before,
    grads,
    table,
    turned_table,
    hub_acc,
    back_acc,
    self_acc,
    neighbor_acc,
    outgoing,
    near,
    part,
    pieces,
    panel,
    arrived,
    hub_terms,
    back_rows,
    b_near,
    b_part,
    b_pieces,
    whole,
    owned,
    owned_near,
    returned,
    weights,
    w_near,
    w_part,
    w_pieces,
    w_across,
    w_block,
    w_whole,
    load_sems,
    *sems,
):
    here = Place()
    depth, groups = here.depth, here.groups
    pairs = [(sems[2 * k], sems[2 * k + 1]) for k in range(len(sems) // 2)]
    lines, _, width = features_ref.shape
    nodes = lines * TILE
    tiles = values_ref.shape[0]
    per_chunk = CHUNK // TILE
    chunks = nodes // CHUNK
    each = mask_ref.shape[0] // ACROSS
    per = depth // each
    sent = []
    loads = []
    for k, (source, target) in enumerate(
        (
            (features_hbm, features_ref),
            (values_hbm, values_ref),
            (cut_hbm, cut_ref),
            (hub_hbm, hub_ref),
            (cotangent_hbm, cotangent_ref),
        )
    ):
        load = pltpu.make_async_copy(source, target, load_sems.at[k])
        load.start()
        loads.append(load)

    def send(*args):
        copies = send_all(*args, pairs[len(sent)])
        sent.append(copies)
        return copies

    def owns(section, row):
        return mask_ref[section, row]

    def chunk_rows(c):
        return pl.ds(pl.multiple_of(c * CHUNK, CHUNK), CHUNK)

    def tile_rows(k):
        return pl.ds(pl.multiple_of(k * TILE, TILE), TILE)

    def own_rows(c):
        return features_ref[pl.ds(c * per_chunk, per_chunk)].reshape(CHUNK, width)

    here.greet()
    heads = features_hbm.at[0]
    heads_out = send(here.along_x, ACROSS, lambda p, d: heads, lambda d: near.at[d - 1])

    loads[0].wait()
    turned_rows = columns_ref[...].T
    count = columns_ref.shape[1]
    for g in range(0, groups, 2):
        picked = jnp.concatenate([turned_rows[:, g : g + 1], turned_rows[:, g + 1 : g + 2]], axis=0)
        spot = lax.broadcasted_iota(jnp.int32, (2 * count, nodes), 1)
        chosen = jnp.where(spot == picked, 1.0, 0.0).astype(BF16)
        table[g * count : (g + 2) * count, :] = chosen
        outgoing[g : g + 2] = dot(chosen, features_ref[...].reshape(nodes, width)).astype(BF16).reshape(2, count, width)
    cut_out = send(
        here.along_grp, groups, lambda p, d: outgoing.at[p], lambda d: arrived.at[here.grp]
    )
    arrived[here.grp] = outgoing[here.grp]

    arrive(heads_out)
    for j in range(each):
        section = here.x * each + j
        total = features_ref[0].astype(F32) * owns(section, here.row)
        for shift in range(1, ACROSS):
            sender = here.z * ACROSS + lax.rem(here.x + ACROSS - shift, ACROSS)
            total += near[shift - 1].astype(F32) * owns(section, sender)
        part[pl.ds(j * per, per)] = total.astype(BF16).reshape(per, HUB // per, width)
    parts_out = send(here.along_z, depth, lambda p, d: part.at[p], lambda d: pieces.at[d - 1])

    loads[1].wait()
    slots[tiles] = jnp.zeros(slots.shape[1:], F32)

    def gather_tile(t, carry):
        slots[t] = slots[links_ref[t]] + dot(values_ref[t], features_ref[index_ref[1, t]])
        return carry

    lax.fori_loop(0, tiles // 2, gather_tile, 0, unroll=4)

    arrive(parts_out)
    total = part[here.z].astype(F32)
    for shift in range(1, depth):
        total += pieces[shift - 1].astype(F32)
    panel[here.x, here.z] = total.astype(BF16)
    mine = panel.at[here.x, here.z]
    pieces_out = send(here.along_z, depth, lambda p, d: mine, lambda d: mine)

    lax.fori_loop(tiles // 2, tiles, gather_tile, 0, unroll=4)

    arrive(pieces_out)
    block = panel.at[here.x]
    panels_out = send(here.along_x, ACROSS, lambda p, d: block, lambda d: block)

    turned_scale = lax.rsqrt(degrees_ref[...].astype(F32)).T
    for k in range(lines):
        scale_ref[k * TILE : (k + 1) * TILE, :] = jnp.broadcast_to(
            turned_scale[:, k : k + 1], (TILE, TILE)
        )
    loads[2].wait()
    arrive(cut_out)

    def begin(c, carry):
        rows = chunk_rows(c)
        total_ref[rows, :] = dot(own_rows(c), self_ref[...])
        inner = dot(cut_ref[rows, :], arrived[...].reshape(-1, width))
        for k in range(per_chunk):
            last = links_ref[tiles + c * per_chunk + k]
            acc[tile_rows(c * per_chunk + k), :] = (
                inner[k * TILE : (k + 1) * TILE] + slots[last]
            )
        return carry

    lax.fori_loop(0, chunks, begin, 0)
    self_acc[...] = jnp.zeros_like(self_acc)
    neighbor_acc[...] = jnp.zeros_like(neighbor_acc)
    hub_acc[...] = jnp.zeros_like(hub_acc)
    back_acc[...] = jnp.zeros_like(back_acc)
    loads[3].wait()
    loads[4].wait()
    arrive(panels_out)

    def spread_scale(rows):
        scale = scale_ref[rows, :]
        return jnp.concatenate([scale] * (width // TILE), axis=1)

    def forward(c, carry):
        rows = chunk_rows(c)
        gathered = acc[rows, :] + dot(hub_ref[rows, :], panel[...].reshape(-1, width))
        aggregated = (gathered * spread_scale(rows)).astype(BF16)
        before = total_ref[rows, :] + dot(aggregated, neighbor_ref[...])
        root = 0.7978845608028654
        square = before * before
        bend = jnp.tanh(root * before * (1.0 + 0.044715 * square))
        half = 0.5 * (1.0 + bend)
        both_ref[0, rows, :] = (before * half).astype(BF16)
        slope = half + 0.5 * before * (1.0 - bend * bend) * (
            root * (1.0 + 3.0 * 0.044715 * square)
        )
        grad_before = (cotangent_ref[rows, :].astype(F32) * slope).astype(BF16)
        grads_before[rows, :] = grad_before
        turned = grad_before.T
        self_acc[...] += dot(turned, own_rows(c))
        neighbor_acc[...] += dot(turned, aggregated)
        return carry

    lax.fori_loop(0, chunks, forward, 0)
    weights[: groups // 2] = self_acc[...].T.reshape(groups // 2, -1, width)
    weights[groups // 2 :] = neighbor_acc[...].T.reshape(groups // 2, -1, width)
    weight_out = send(
        here.along_grp, groups, lambda p, d: weights.at[p], lambda d: w_near.at[d - 1]
    )

    def backward(c, carry):
        rows = chunk_rows(c)
        grad_aggregate = (
            dot_cols(grads_before[rows, :], neighbor_ref[...]) * spread_scale(rows)
        ).astype(BF16)
        turned = grad_aggregate.T
        for k in range(per_chunk):
            grads[c * per_chunk + k] = turned[:, k * TILE : (k + 1) * TILE]
        hub_acc[...] += dot(turned, hub_ref[rows, :])
        back_acc[...] += dot(turned, cut_ref[rows, :])
        return carry

    lax.fori_loop(0, chunks, backward, 0)
    hub_terms[...] = hub_acc[...].T.astype(BF16).reshape(hub_terms.shape)
    hub_out = send(
        here.along_x, ACROSS, lambda p, d: hub_terms.at[p], lambda d: b_near.at[d - 1]
    )
    back_rows[...] = back_acc[...].T.astype(BF16).reshape(back_rows.shape)
    back_out = send(
        here.along_grp, groups, lambda p, d: back_rows.at[p], lambda d: returned.at[here.grp]
    )
    returned[here.grp] = back_rows[here.grp]

    arrive(weight_out)
    total = weights[here.grp]
    for shift in range(1, groups):
        total += w_near[shift - 1]
    w_part[...] = total.reshape(w_part.shape)
    w_parts_out = send(
        here.along_z, depth, lambda p, d: w_part.at[p], lambda d: w_pieces.at[d - 1]
    )

    sides[tiles] = jnp.zeros(sides.shape[1:], F32)
    base = tiles + lines

    def return_tile(t, carry):
        sides[t] = sides[links_ref[base + t]] + dot(grads[index_ref[0, t]], values_ref[t])
        return carry

    lax.fori_loop(0, tiles // 2, return_tile, 0, unroll=4)

    arrive(hub_out)
    total = hub_terms[here.x].astype(F32)
    for shift in range(1, ACROSS):
        total += b_near[shift - 1].astype(F32)
    b_part[...] = total.astype(BF16).reshape(b_part.shape)
    b_parts_out = send(
        here.along_z, depth, lambda p, d: b_part.at[p], lambda d: b_pieces.at[d - 1]
    )

    arrive(w_parts_out)
    total = w_part[here.z]
    for shift in range(1, depth):
        total += w_pieces[shift - 1]
    w_across[here.x] = total
    w_mine = w_across.at[here.x]
    w_across_out = send(here.along_x, ACROSS, lambda p, d: w_mine, lambda d: w_mine)

    lax.fori_loop(tiles // 2, tiles, return_tile, 0, unroll=4)

    arrive(w_across_out)
    total = w_across[0]
    for k in range(1, ACROSS):
        total += w_across[k]
    w_block[here.z] = total
    w_piece = w_block.at[here.z]
    w_block_out = send(here.along_z, depth, lambda p, d: w_piece, lambda d: w_piece)

    arrive(b_parts_out)
    total = b_part[here.z].astype(F32)
    for shift in range(1, depth):
        total += b_pieces[shift - 1].astype(F32)
    whole[here.z] = total.astype(BF16)
    whole_mine = whole.at[here.z]
    whole_out = send(here.along_z, depth, lambda p, d: whole_mine, lambda d: whole_mine)

    def collect(c, carry):
        rows = chunk_rows(c)
        inner = dot_cols(grads_before[rows, :], self_ref[...])
        for k in range(per_chunk):
            last = links_ref[base + tiles + c * per_chunk + k]
            total_ref[tile_rows(c * per_chunk + k), :] = (
                inner[k * TILE : (k + 1) * TILE] + sides[last].T
            )
        turned_table[rows, :] = table[:, rows].T
        return carry

    lax.fori_loop(0, chunks, collect, 0)

    arrive(w_block_out)
    w_whole[here.grp] = w_block[...].reshape(w_whole.shape[1:])
    w_last = w_whole.at[here.grp]
    w_whole_out = send(here.along_grp, groups, lambda p, d: w_last, lambda d: w_last)

    def owned_by(row):
        total = jnp.zeros((HUB, width), F32)
        for j in range(each):
            terms = whole[pl.ds(j * per, per)].astype(F32).reshape(HUB, width)
            total += terms * owns(here.x * each + j, row)
        return total

    arrive(whole_out)
    for shift in range(1, ACROSS):
        peer = here.z * ACROSS + lax.rem(here.x + shift, ACROSS)
        owned[shift - 1] = owned_by(peer).astype(BF16)
    owned_out = send(
        here.along_x, ACROSS, lambda p, d: owned.at[d - 1], lambda d: owned_near.at[d - 1]
    )
    arrive(back_out)

    def scatter(c, carry):
        rows = chunk_rows(c)
        total_ref[rows, :] += dot(turned_table[rows, :], returned[...].reshape(-1, width))
        both_ref[1, rows, :] = total_ref[rows, :].astype(BF16)
        return carry

    lax.fori_loop(0, chunks, scatter, 0)

    arrive(owned_out)
    total = owned_by(here.row)
    for shift in range(1, ACROSS):
        total += owned_near[shift - 1].astype(F32)
    both_ref[1, :HUB, :] = (total_ref[:HUB, :] + total).astype(BF16)
    arrive(w_whole_out)
    sum_ref[...] = w_whole[...]
    for copies in sent:
        for copy in copies:
            copy.wait_send()


def pair_sems(*counts):
    return [pltpu.SemaphoreType.DMA((n - 1,)) for n in counts for _ in range(2)]


def shape(dims, dtype):
    return jax.ShapeDtypeStruct(dims, dtype)


def on_device(
    features,
    cotangent,
    self_weight,
    neighbor_weight,
    tile_values,
    tile_index,
    hub_adjacency,
    hub_owner,
    send_rows,
    cut_adjacency,
    degrees,
):
    nodes, width = features.shape
    lines = nodes // TILE
    tiles = tile_values.shape[1]
    groups = lax.axis_size("grp")
    depth = lax.axis_size("row") // ACROSS
    sections = hub_owner.shape[1]
    sent = send_rows.shape[2]
    arrivals = groups * sent
    block = sections // ACROSS * HUB
    piece = block // depth
    wide = 2 * width // groups
    thin = wide // depth
    index = tile_index[0].T

    links, mask = pl.pallas_call(
        chain_tiles,
        out_shape=(
            shape((2 * (tiles + lines),), jnp.int32),
            shape((sections, lax.axis_size("row")), F32),
        ),
        in_specs=[SMEM, SMEM],
        out_specs=(SMEM, SMEM),
        name="chain_tiles",
    )(index, hub_owner)

    def half(*dims):
        return pltpu.VMEM(dims, BF16)

    def full(*dims):
        return pltpu.VMEM(dims, F32)

    both, weights = pl.pallas_call(
        sage_kernel,
        out_shape=(
            shape((2, nodes, width), BF16),
            shape((groups, wide, width), F32),
        ),
        in_specs=[SMEM] * 3 + [VMEM] * 4 + [pl.BlockSpec(memory_space=pl.ANY)] * 5,
        out_specs=(VMEM,) * 2,
        scratch_shapes=[
            half(lines, TILE, width),
            half(nodes, width),
            half(tiles, TILE, TILE),
            half(nodes, sections * HUB),
            half(nodes, arrivals),
            full(nodes, TILE),
            full(nodes, width),
            full(tiles + 1, TILE, width),
            full(tiles + 1, width, TILE),
            full(nodes, width),
            half(nodes, width),
            half(lines, width, TILE),
            half(arrivals, nodes),
            half(nodes, arrivals),
            full(width, sections * HUB),
            full(width, arrivals),
            full(width, width),
            full(width, width),
            half(groups, sent, width),
            half(ACROSS - 1, HUB, width),
            half(depth, piece, width),
            half(depth - 1, piece, width),
            half(ACROSS, depth, piece, width),
            half(groups, sent, width),
            half(ACROSS, block, width),
            half(groups, sent, width),
            half(ACROSS - 1, block, width),
            half(depth, piece, width),
            half(depth - 1, piece, width),
            half(depth, piece, width),
            half(ACROSS - 1, HUB, width),
            half(ACROSS - 1, HUB, width),
            half(groups, sent, width),
            full(groups, wide, width),
            full(groups - 1, wide, width),
            full(depth, thin, width),
            full(depth - 1, thin, width),
            full(ACROSS, thin, width),
            full(depth, thin, width),
            full(groups, wide, width),
            pltpu.SemaphoreType.DMA((5,)),
            *pair_sems(ACROSS, groups, depth, depth, ACROSS),
            *pair_sems(
                groups, ACROSS, groups, depth, depth, ACROSS, depth, depth, groups, ACROSS
            ),
        ],
        compiler_params=pltpu.CompilerParams(
            collective_id=0, has_side_effects=True, vmem_limit_bytes=60 * 1024 * 1024
        ),
        name="sage",
    )(
        index,
        links,
        mask,
        send_rows[0],
        degrees.reshape(lines, TILE),
        self_weight,
        neighbor_weight,
        features.reshape(lines, TILE, width),
        cotangent,
        tile_values[0],
        hub_adjacency,
        cut_adjacency,
    )
    weights = weights.reshape(2 * width, width)
    return (both[0], both[1], weights[:width], weights[width:])


def solution(mesh):
    in_specs = (
        P(("grp", "row"), None),
        P(("grp", "row"), None),
        P(),
        P(),
        P(("grp", "row"), None, None, None),
        P(("grp", "row"), None, None),
        P(("grp", "row"), None),
        P("grp", None),
        P(("grp", "row"), None, None),
        P(("grp", "row"), None),
        P(("grp", "row")),
    )
    out_specs = (P(("grp", "row"), None), P(("grp", "row"), None), P(), P())
    return jax.shard_map(
        on_device, mesh=mesh, in_specs=in_specs, out_specs=out_specs, check_vma=False
    )
```

time: 640 us -> 79.7 us (0.12)
  waiting for transfers between devices: 490 us -> 0 us
  Pallas kernels: 0 us -> 75 us
  matrix products: 58.4 us -> 0 us
  local copies, waits for them, and re-layouts: 46.5 us -> 3.89 us
  between operations: 19 us -> 0.66 us
  starting transfers between devices: 16.3 us -> 0 us
    psum x3 -> x0, waiting for transfers between devices: 490 us -> none  [the longest x1 232 us: on_device(): lax.psum((self_part, neighbor_part), ('grp', 'row'))]
    pallas_call x0 -> x2, Pallas kernels: none -> 75 us  [the longest x1 72.8 us: on_device(): pl.pallas_call(sage_kernel, out_shape=(shape((2, nodes, width), BF16), sh...]
    dot_general x23 -> x0, matrix products: 58.4 us -> none  [the longest x8 7.35 us: on_device(): jnp.dot(hub_adjacency[:, section * HUB:(section + 1) * HUB], panel, prefe...]
    dot_general x5 -> x0, local copies, waits for them, and re-layouts: 23.7 us -> none  [the longest x1 9.22 us: on_device(): jnp.einsum('lab,lbf->laf', values, picked, preferred_element_type=jnp.flo...]
    all_to_all x2 -> x0, starting transfers between devices: 16.2 us -> none  [the longest x1 9.67 us: on_device(): lax.all_to_all(back_rows, 'grp', split_axis=0, concat_axis=0, tiled=True)]
    gather x3 -> x0, local copies, waits for them, and re-layouts: 9.2 us -> none  [the longest x1 3.59 us: on_device(): outgoing = features[send_rows[0]]]
    unnamed x53 -> x2, local copies, waits for them, and re-layouts: 6.73 us -> 0.01 us
  transfers between devices with their start and end apart: 5 -> 0, of which waited for: 3 -> 0; matrix products, arithmetic and copies ran while one was open for 9% -> 0% of each run, Pallas kernels for 0% -> 0%
where the time goes in v2:
time: 79.7 us; the launch traced here: 79.6 us
  Pallas kernels  75 us (94%)
  local copies, waits for them, and re-layouts  3.89 us (5%)
    pallas_call x1, Pallas kernels, on_device(): pl.pallas_call(sage_kernel, out_shape=(shape((2, nodes, width), BF16), sh...  72.8 us
    squeeze x1, local copies, waits for them, and re-layouts, on_device(): return (both[0], both[1], weights[:width], weights[width:])  3.05 us
    pallas_call x1, Pallas kernels, on_device(): pl.pallas_call(chain_tiles, out_shape=(shape((2 * (tiles + lines),), jnp....  2.24 us

profile of v2, /device:TPU:1, one launch (start us, length us, event | category | flops | bytes accessed | tf_op | source)
XLA Modules:
  0.0 79.6 jit_solution(12782956879214674764)
XLA Ops:
  0.6 2.2 %chain_tiles.1 = (s32[160]{0:T(256)}, f32[8,32]{1,0:T(8,128)}) custom-call(s32[2,64]{1,0:T(2,128)} %bitcast.19, s32[1,8]{1,0:T(1,128)} %owner_ref.1), custom_call_target="tpu_custom_call" | custom-call | tf_op jit(solution)/shard_map/chain_tiles/pallas_call | solution.py:494
  2.9 72.8 %sage.1 = (bf16[2,2048,256]{2,1,0:T(8,128)(2,1)}, f32[8,64,256]{2,1,0:T(8,128)}) custom-call(s32[2,64]{1,0:T(2,128)} %bitcast.20, s32[160]{0:T(256)} %get-tuple-element.8.links_ref, f32[8,32]{1,0:T(8,128)} %get-tuple-element.9.mask_ref, s32[8,64]{1,0:T(8,128)} %bitcast.18, s32[16,128]{1,0:T(8,128)} %bitcast.17, bf16[256,256]{1,0:T(8,128)(2,1)} %self_ref.1, ...), custom_call_target="tpu_custom_call" | custom-call | tf_op jit(solution)/shard_map/sage/pallas_call | solution.py:511
  75.7 0.0 copy-start
  75.7 3.0 %slice_bitcast_fusion = (bf16[2048,256]{1,0:T(8,128)(2,1)}, bf16[2048,256]{1,0:T(8,128)(2,1)}) fusion(bf16[2,2048,256]{2,1,0:T(8,128)(2,1)} %get-tuple-element.10), kind=kLoop, calls=%fused_computation | loop fusion | bytes 4194304 | tf_op jit(solution)/shard_map/squeeze | solution.py:585
  78.7 0.0 copy-done
  78.7 0.8 %fusion = (f32[4,64,256]{2,1,0:T(8,128)}, f32[4,64,256]{2,1,0:T(8,128)}) fusion(f32[8,64,256]{2,1,0:T(8,128)S(1)} %copy-done), kind=kLoop, calls=%fused_computation.2 | loop fusion | bytes 1048576 | tf_op jit(solution)/shard_map/slice | solution.py:585
Async XLA Ops:
  75.7 3.1 %copy-start = (f32[8,64,256]{2,1,0:T(8,128)S(1)}, f32[8,64,256]{2,1,0:T(8,128)}, u32[]{:S(2)}) copy-start(f32[8,64,256]{2,1,0:T(8,128)} %get-tuple-element.11) | copy-start | bytes 1572868

commit v3 on v2

--- a/solution.py
+++ b/solution.py
@@ -169,7 +169,6 @@
     w_part,
     w_pieces,
     w_across,
-    w_block,
     w_whole,
     load_sems,
     *sems,
@@ -260,12 +259,14 @@
     panel[here.x, here.z] = total.astype(BF16)
     mine = panel.at[here.x, here.z]
     pieces_out = send(here.along_z, depth, lambda p, d: mine, lambda d: mine)
+    panels_out = send(here.along_x, ACROSS, lambda p, d: mine, lambda d: mine)
 
     lax.fori_loop(tiles // 2, tiles, gather_tile, 0, unroll=4)
 
-    arrive(pieces_out)
-    block = panel.at[here.x]
-    panels_out = send(here.along_x, ACROSS, lambda p, d: block, lambda d: block)
+    for shift in nearest(depth):
+        pieces_out[shift - 1].wait_recv()
+        piece = panel.at[here.x, lax.rem(here.z + depth - shift, depth)]
+        panels_out = panels_out + send(here.along_x, ACROSS, lambda p, d: piece, lambda d: piece)
 
     turned_scale = lax.rsqrt(degrees_ref[...].astype(F32)).T
     for k in range(lines):
@@ -390,9 +391,10 @@
     total = w_across[0]
     for k in range(1, ACROSS):
         total += w_across[k]
-    w_block[here.z] = total
-    w_piece = w_block.at[here.z]
-    w_block_out = send(here.along_z, depth, lambda p, d: w_piece, lambda d: w_piece)
+    w_whole[here.grp, here.z] = total
+    w_own = w_whole.at[here.grp, here.z]
+    w_block_out = send(here.along_z, depth, lambda p, d: w_own, lambda d: w_own)
+    w_whole_out = send(here.along_grp, groups, lambda p, d: w_own, lambda d: w_own)
 
     arrive(b_parts_out)
     total = b_part[here.z].astype(F32)
@@ -413,12 +415,16 @@
         turned_table[rows, :] = table[:, rows].T
         return carry
 
-    lax.fori_loop(0, chunks, collect, 0)
-
-    arrive(w_block_out)
-    w_whole[here.grp] = w_block[...].reshape(w_whole.shape[1:])
-    w_last = w_whole.at[here.grp]
-    w_whole_out = send(here.along_grp, groups, lambda p, d: w_last, lambda d: w_last)
+    lax.fori_loop(0, chunks // 2, collect, 0)
+
+    for shift in nearest(depth):
+        w_block_out[shift - 1].wait_recv()
+        w_piece = w_whole.at[here.grp, lax.rem(here.z + depth - shift, depth)]
+        w_whole_out = w_whole_out + send(
+            here.along_grp, groups, lambda p, d: w_piece, lambda d: w_piece
+        )
+
+    lax.fori_loop(chunks // 2, chunks, collect, 0)
 
     def owned_by(row):
         total = jnp.zeros((HUB, width), F32)
@@ -450,10 +456,14 @@
         total += owned_near[shift - 1].astype(F32)
     both_ref[1, :HUB, :] = (total_ref[:HUB, :] + total).astype(BF16)
     arrive(w_whole_out)
-    sum_ref[...] = w_whole[...]
+    sum_ref[...] = w_whole[...].reshape(sum_ref.shape)
     for copies in sent:
         for copy in copies:
             copy.wait_send()
+
+
+def nearest(size):
+    return sorted(range(1, size), key=lambda shift: min(shift, size - shift))
 
 
 def pair_sems(*counts):
@@ -555,13 +565,11 @@
             full(depth, thin, width),
             full(depth - 1, thin, width),
             full(ACROSS, thin, width),
-            full(depth, thin, width),
-            full(groups, wide, width),
+            full(groups, depth, thin, width),
             pltpu.SemaphoreType.DMA((5,)),
-            *pair_sems(ACROSS, groups, depth, depth, ACROSS),
-            *pair_sems(
-                groups, ACROSS, groups, depth, depth, ACROSS, depth, depth, groups, ACROSS
-            ),
+            *pair_sems(ACROSS, groups, depth, depth, *[ACROSS] * depth),
+            *pair_sems(groups, ACROSS, groups, depth, depth, ACROSS, depth, groups, depth),
+            *pair_sems(*[groups] * (depth - 1), ACROSS),
         ],
         compiler_params=pltpu.CompilerParams(
             collective_id=0, has_side_effects=True, vmem_limit_bytes=60 * 1024 * 1024

time: 79.7 us -> 77.3 us (0.970)
  Pallas kernels: 75 us -> 72.1 us
    pallas_call x1, Pallas kernels: 72.8 us -> 69.8 us  [on_device(): pl.pallas_call(sage_kernel, out_shape=(shape((2, nodes, width), BF16), sh...]
where the time goes in v3:
time: 77.3 us; the launch traced here: 76.6 us
  Pallas kernels  72.1 us (93%)
  local copies, waits for them, and re-layouts  3.89 us (5%)
    pallas_call x1, Pallas kernels, on_device(): pl.pallas_call(sage_kernel, out_shape=(shape((2, nodes, width), BF16), sh...  69.8 us
    squeeze x1, local copies, waits for them, and re-layouts, on_device(): return (both[0], both[1], weights[:width], weights[width:])  3.05 us
    pallas_call x1, Pallas kernels, on_device(): pl.pallas_call(chain_tiles, out_shape=(shape((2 * (tiles + lines),), jnp....  2.24 us

profile of v3, /device:TPU:1, one launch (start us, length us, event | category | flops | bytes accessed | tf_op | source)
XLA Modules:
  0.0 76.6 jit_solution(14371639701462187860)
XLA Ops:
  0.6 2.2 %chain_tiles.1 = (s32[160]{0:T(256)}, f32[8,32]{1,0:T(8,128)}) custom-call(s32[2,64]{1,0:T(2,128)} %bitcast.19, s32[1,8]{1,0:T(1,128)} %owner_ref.1), custom_call_target="tpu_custom_call" | custom-call | tf_op jit(solution)/shard_map/chain_tiles/pallas_call | solution.py:504
  2.9 69.8 %sage.1 = (bf16[2,2048,256]{2,1,0:T(8,128)(2,1)}, f32[8,64,256]{2,1,0:T(8,128)}) custom-call(s32[2,64]{1,0:T(2,128)} %bitcast.20, s32[160]{0:T(256)} %get-tuple-element.8.links_ref, f32[8,32]{1,0:T(8,128)} %get-tuple-element.9.mask_ref, s32[8,64]{1,0:T(8,128)} %bitcast.18, s32[16,128]{1,0:T(8,128)} %bitcast.17, bf16[256,256]{1,0:T(8,128)(2,1)} %self_ref.1, ...), custom_call_target="tpu_custom_call" | custom-call | tf_op jit(solution)/shard_map/sage/pallas_call | solution.py:521
  72.7 0.0 copy-start
  72.7 3.0 %slice_bitcast_fusion = (bf16[2048,256]{1,0:T(8,128)(2,1)}, bf16[2048,256]{1,0:T(8,128)(2,1)}) fusion(bf16[2,2048,256]{2,1,0:T(8,128)(2,1)} %get-tuple-element.10), kind=kLoop, calls=%fused_computation | loop fusion | bytes 4194304 | tf_op jit(solution)/shard_map/squeeze | solution.py:593
  75.8 0.0 copy-done
  75.8 0.8 %fusion = (f32[4,64,256]{2,1,0:T(8,128)}, f32[4,64,256]{2,1,0:T(8,128)}) fusion(f32[8,64,256]{2,1,0:T(8,128)S(1)} %copy-done), kind=kLoop, calls=%fused_computation.2 | loop fusion | bytes 1048576 | tf_op jit(solution)/shard_map/slice | solution.py:593
Async XLA Ops:
  72.7 3.1 %copy-start = (f32[8,64,256]{2,1,0:T(8,128)S(1)}, f32[8,64,256]{2,1,0:T(8,128)}, u32[]{:S(2)}) copy-start(f32[8,64,256]{2,1,0:T(8,128)} %get-tuple-element.11) | copy-start | bytes 1572868
